TPU v7x, 256 devices: a whole 4x4x8 slice. The times are simulated.
256 devices in a mesh: ctx: 32 (over y, z), tp: 8 (over x, core).
Axes of the slice: x: 4, y: 4, z: 8, core: 2. Of those that a mesh axis runs over, the one named last changes fastest.
Arguments:
- ssm_inputs: bfloat16 [8192, 8192], P('ctx', 'tp'), may hold values from -4 to 4
- state_maps: bfloat16 [8192, 8, 256], P('ctx', 'tp'), may hold values from -4 to 4
- ssm_gates: bfloat16 [8192, 8192], P('ctx', 'tp'), may hold values from -4 to 4
- time_steps: float32 [128, 8192], P('tp', 'ctx'), may hold values from -5 to 512
- log_rates: float32 [128], P('tp'), may hold values from -12 to 1
- skip_gain: float32 [128], P('tp'), may hold values from 0.5 to 2
- conv_inputs: bfloat16 [4, 8192], P(None, 'tp'), may hold values from -3 to 3
- conv_maps: bfloat16 [4, 8, 256], P(None, 'tp'), may hold values from -3 to 3
- norm_gain: float32 [8192], P('tp'), may hold values from 0.1 to 1.9
- out_weight: bfloat16 [8192, 4096], P('tp'), may hold values from -0.0625 to 0.0625
- queries: bfloat16 [8192, 8192], P('ctx', 'tp'), may hold values from -5 to 5
- attention_keys: bfloat16 [8192, 1024], P('ctx', 'tp'), may hold values from -5 to 5
- values: bfloat16 [8192, 1024], P('ctx', 'tp'), may hold values from -4 to 4
Outputs:
- ssm_out: bfloat16 [8192, 4096], P(('ctx', 'tp'))
- attn_out: bfloat16 [8192, 8192], P('ctx', 'tp')
All inputs are finite; a program needn't handle non-finite values.
Results may differ from a plain program's by a relative error of at most 0.03.
Values may be sent and summed in bfloat16 or wider, within the bound.
No kernel may reach another device: no remote copies, remote signals or barrier semaphores. Data moves between devices by JAX's collectives and lax.ppermute only.
A program may use at most 128 MiB of HBM per device.

v0:
```python
import jax
import jax.numpy as jnp
from jax import lax
from jax.sharding import PartitionSpec as P

QUERY_HEADS = 64
KEY_VALUE_HEADS = 8
HEAD_SIZE = 128


def passed_along(shard, axis, by):
    size = lax.axis_size(axis)
    pairs = [(i, i + by) for i in range(size) if 0 <= i + by < size]
    return lax.ppermute(shard, axis, pairs)


def prefix_2(shard, axis, join, neutral):
    place = lax.axis_index(axis)
    gathered = jax.tree.map(
        lambda a, kind: lax.all_gather(a.astype(kind), axis), shard, (jnp.bfloat16, jnp.bfloat16)
    )
    state = jax.tree.map(lambda a, e: jnp.zeros_like(a) + jnp.asarray(e, a.dtype), shard, neutral)

    def one(step, state):
        return join(
            state,
            jax.tree.map(
                lambda a, own: lax.dynamic_index_in_dim(a, step, 0, False).astype(own.dtype),
                gathered,
                shard,
            ),
        )

    return lax.fori_loop(0, place, one, state)


def conv_silu(extended, conv_taps, tok_rows):
    summed = jnp.zeros((tok_rows,) + extended.shape[1:], jnp.float32)
    for tap_index in range(conv_taps.shape[0]):
        summed = summed + conv_taps[tap_index].astype(jnp.float32) * extended[
            tap_index : tap_index + tok_rows
        ].astype(jnp.float32)
    return jax.nn.silu(summed).astype(jnp.bfloat16)


def per_device(
    ssm_inputs,
    state_maps,
    ssm_gates,
    time_steps,
    log_rates,
    skip_gain,
    conv_inputs,
    conv_maps,
    norm_gain,
    out_weight,
    queries,
    attention_keys,
    values,
):
    tok_rows = ssm_inputs.shape[0]
    tap_count = conv_inputs.shape[0]
    groups_here = state_maps.shape[1]
    state_size = state_maps.shape[2] // 2
    heads_here = log_rates.shape[0]
    per_group = heads_here // groups_here
    head_dim = ssm_inputs.shape[1] // heads_here
    my_index = lax.axis_index("ctx")
    lead_inputs, lead_maps = passed_along(
        (ssm_inputs[tok_rows - tap_count + 1 :], state_maps[tok_rows - tap_count + 1 :]), "ctx", 1
    )
    mixed_inputs = conv_silu(
        jnp.concatenate([lead_inputs, ssm_inputs], axis=0), conv_inputs, tok_rows
    )
    mixed_maps = conv_silu(jnp.concatenate([lead_maps, state_maps], axis=0), conv_maps, tok_rows)
    input_heads = mixed_inputs.reshape(tok_rows, groups_here, per_group, head_dim)
    b_maps = mixed_maps[:, :, :state_size]
    c_maps = mixed_maps[:, :, state_size:]
    step_sizes = jax.nn.softplus(time_steps).reshape(groups_here, per_group, tok_rows)
    decline_rate = -jnp.exp(log_rates).reshape(groups_here, per_group)
    running_log = jnp.cumsum(step_sizes * decline_rate[:, :, None], axis=2)
    map_products = jnp.einsum("tgn,sgn->gts", c_maps, b_maps, preferred_element_type=jnp.float32)
    token_location = jnp.arange(tok_rows)
    causal = token_location[:, None] >= token_location[None, :]
    log_gap = running_log[:, :, :, None] - running_log[:, :, None, :]
    decay_table = jnp.where(causal, jnp.exp(jnp.minimum(log_gap, 0.0)), 0.0)
    mixer = (map_products[:, None] * decay_table * step_sizes[:, :, None, :]).astype(jnp.bfloat16)
    inner_part = jnp.einsum(
        "gjts,sgjp->tgjp", mixer, input_heads, preferred_element_type=jnp.float32
    )
    inputs_float = input_heads.astype(jnp.float32)
    tail_weight = jnp.exp(running_log[:, :, -1:] - running_log) * step_sizes
    weighted = (jnp.transpose(tail_weight, (2, 0, 1))[..., None] * inputs_float).astype(
        jnp.bfloat16
    )
    block_state = jnp.einsum("sgjp,sgn->gjpn", weighted, b_maps, preferred_element_type=jnp.float32)
    block_decay = running_log[:, :, -1]

    def combine(earlier, later):
        return (earlier[0] + later[0], jnp.exp(later[0])[:, :, None, None] * earlier[1] + later[1])

    prefix = prefix_2(
        (block_decay, block_state),
        "ctx",
        combine,
        (jnp.zeros_like(block_decay), jnp.zeros_like(block_state)),
    )
    entering = prefix[1]
    carried = jnp.einsum(
        "tgn,gjpn->tgjp", c_maps.astype(jnp.float32), entering, precision=lax.Precision.HIGHEST
    )
    outside = jnp.transpose(jnp.exp(running_log), (2, 0, 1))[..., None] * carried
    ssm_output = (
        inner_part
        + outside
        + skip_gain.reshape(groups_here, per_group)[None, :, :, None] * inputs_float
    )
    channel_count = per_group * head_dim
    gated = ssm_output.reshape(tok_rows, groups_here, channel_count) * jax.nn.silu(
        ssm_gates.reshape(tok_rows, groups_here, channel_count).astype(jnp.float32)
    )
    mean_square = jnp.mean(gated * gated, axis=2, keepdims=True)
    normed = (
        (gated * lax.rsqrt(mean_square + 1e-05)).reshape(tok_rows, groups_here * channel_count)
        * norm_gain
    ).astype(jnp.bfloat16)
    ssm_out = lax.psum_scatter(
        jnp.dot(normed, out_weight, preferred_element_type=jnp.float32).astype(jnp.bfloat16),
        "tp",
        scatter_dimension=0,
        tiled=True,
    )
    kv_heads = attention_keys.shape[1] // HEAD_SIZE
    shared_heads = QUERY_HEADS // KEY_VALUE_HEADS
    score_scale = HEAD_SIZE ** (-0.5)
    query_pos = my_index * tok_rows + token_location
    query_heads = queries.reshape(tok_rows, kv_heads, shared_heads, HEAD_SIZE)
    block_rows = tok_rows // 4
    first_key = jnp.int32(0)
    key_block = lax.all_gather(attention_keys, "ctx", axis=0, tiled=True)
    value_block = lax.all_gather(values, "ctx", axis=0, tiled=True)
    key_count = key_block.shape[0]
    key_head_rows = key_block.reshape(key_count, kv_heads, HEAD_SIZE)
    value_head_rows = value_block.reshape(key_count, kv_heads, HEAD_SIZE)
    key_pos = jnp.arange(key_count)
    peaks = jnp.full((kv_heads, shared_heads, tok_rows), -1e30, jnp.float32)
    totals = jnp.zeros((kv_heads, shared_heads, tok_rows), jnp.float32)
    sums = jnp.zeros((kv_heads, shared_heads, tok_rows, HEAD_SIZE), jnp.float32)
    new_parts = []
    for current_block_index in range(4):
        row_lower = current_block_index * block_rows
        row_upper = row_lower + block_rows
        query_tile_block = query_heads[row_lower:row_upper]
        block_pos = query_pos[row_lower:row_upper]
        old_state = (
            peaks[:, :, row_lower:row_upper],
            totals[:, :, row_lower:row_upper],
            sums[:, :, row_lower:row_upper],
        )

        def update(old_part, query_tile_block=query_tile_block, block_pos=block_pos):
            old_peak, old_total, old_sum = old_part
            scores = (
                jnp.einsum(
                    "bgrd,kgd->grbk",
                    query_tile_block,
                    key_head_rows,
                    preferred_element_type=jnp.float32,
                )
                * score_scale
            )
            allowed = key_pos[None, :] <= block_pos[:, None]
            scores = jnp.where(allowed, scores, -1e30)
            new_peak = jnp.maximum(old_peak, jnp.max(scores, axis=3))
            weights = jnp.where(allowed, jnp.exp(scores - new_peak[..., None]), 0.0)
            new_total = jnp.sum(weights, axis=3)
            new_sum = jnp.einsum(
                "grbk,kgd->grbd",
                weights.astype(jnp.bfloat16),
                value_head_rows,
                preferred_element_type=jnp.float32,
            )
            return (new_peak, new_total, new_sum)

        def unchanged(old_part):
            return old_part

        new_parts.append(
            lax.cond(block_pos[block_rows - 1] >= first_key, update, unchanged, old_state)
        )
    peaks, totals, sums = tuple(
        (
            jnp.concatenate([block_part[member] for block_part in new_parts], axis=2)
            for member in range(3)
        )
    )
    attended = sums / totals[..., None]
    attn_out = (
        jnp.transpose(attended, (2, 0, 1, 3))
        .reshape(tok_rows, kv_heads * shared_heads * HEAD_SIZE)
        .astype(jnp.bfloat16)
    )
    return (ssm_out, attn_out)


def solution(mesh):
    placed = (
        P("ctx", "tp"),
        P("ctx", "tp", None),
        P("ctx", "tp"),
        P("tp", "ctx"),
        P("tp"),
        P("tp"),
        P(None, "tp"),
        P(None, "tp", None),
        P("tp"),
        P("tp", None),
        P("ctx", "tp"),
        P("ctx", "tp"),
        P("ctx", "tp"),
    )
    return jax.shard_map(
        per_device,
        mesh=mesh,
        in_specs=placed,
        out_specs=(P(("ctx", "tp"), None), P("ctx", "tp")),
        check_vma=False,
    )
```

profile of v0, /device:TPU:4, one launch (start us, length us, event | category | flops | bytes accessed | tf_op | source)
XLA Modules:
  0.0 351.8 jit_solution(560110108480496360)
XLA Ops:
  7.2 0.7 slice.117
  8.2 3.8 %collective-permute-start = (bf16[3,1024]{0,1:T(8,128)(2,1)S(1)}, bf16[3,1024]{0,1:T(8,128)(2,1)S(1)}, u32[]{:S(2)}, u32[]{:S(2)}) collective-permute-start(bf16[3,1024]{0,1:T(8,128)(2,1)S(1)} %copy.76), channel_id=1, source_target_pairs={{0,8},{8,16},{16,24},{24,32},{32,40},{40,48},{48,56},{56,64},{64,7... | collective-permute-start | bytes 18440 | tf_op jit(solution)/shard_map/ppermute | solution.py:14
  12.0 0.7 slice.125
  12.7 3.8 %collective-permute-start.1 = (bf16[3,1,256]{2,0,1:T(4,128)(2,1)S(1)}, bf16[3,1,256]{2,0,1:T(4,128)(2,1)S(1)}, u32[]{:S(2)}, u32[]{:S(2)}) collective-permute-start(bf16[3,1,256]{2,0,1:T(4,128)(2,1)S(1)} %slice.125), channel_id=1, source_target_pairs={{0,8},{8,16},{16,24},{24,32},{32,40},{40,48},{48,56},{56,64},{64,7... | collective-permute-start | bytes 4616 | tf_op jit(solution)/shard_map/ppermute | solution.py:14
  16.5 0.7 exponential_negate_fusion
  17.2 0.8 compare_select_fusion
  18.0 0.6 reduce-window.6
  19.0 0.9 slice_convert_fusion.3
  19.9 0.8 multiply_bitcast_fusion
  20.7 0.8 slice_convert_fusion.7
  21.6 1.2 copy.77
  22.8 1.4 multiply_convert_fusion.7
  24.3 1.5 fusion.96
  25.7 1.0 convolution_convert_fusion.1
  26.8 0.7 all-gather.6.cloned.1.call-update
  27.6 0.7 all-gather.8.cloned.1.call-update
  28.3 40.3 %all-gather = bf16[32,16,1]{1,2,0:T(2,128)(2,1)S(1)} all-gather(bf16[1,16,1]{1,2,0:T(2,128)(2,1)S(1)} %slice.213), channel_id=2, replica_groups=mesh['ctx'=32,'tp'=8] {'ctx'}, dimensions={0}, use_global_device_ids=true | all-gather | bytes 1056 | tf_op jit(solution)/shard_map/all_gather | solution.py:20
  68.9 1.3 copy.88
  70.4 1.4 fusion.87
  71.8 54.2 %all-gather.10.cloned.1.call-done = bf16[512,64,128]{2,1,0:T(8,128)(2,1)} async-done(((bf16[16,64,128]{2,1,0:T(8,128)(2,1)}), bf16[512,64,128]{2,1,0:T(8,128)(2,1)}) %all-gather.10.cloned.1.call-update) | async-done | bytes 8388624 | tf_op jit(solution)/shard_map/all_gather | solution.py:20
  126.0 0.6 fusion.90
  126.6 0.4 multiply_reduce_fusion
  127.0 7.2 %convolution_convert_fusion = bf16[256,4096]{1,0:T(8,128)(2,1)} fusion(bf16[1024,4096]{1,0:T(8,128)(2,1)} %param.32, f32[256,1024]{0,1:T(8,128)S(1)} %get-tuple-element.171, f32[1024]{0:T(1024)S(1)} %copy-done, f32[256]{0:T(256)S(1)} %add_rsqrt_fusion), kind=kOutput, calls=%fused_computation.82 | convolution fusion | flops 2149318656 | bytes 11539456 | tf_op jit(solution)/shard_map/dot_general | solution.py:128
  134.2 0.6 fusion.116
  137.2 66.5 %all-gather.6.cloned.1.call-done = bf16[8192,128]{1,0:T(8,128)(2,1)} async-done(((bf16[256,128]{1,0:T(8,128)(2,1)}), bf16[8192,128]{1,0:T(8,128)(2,1)}) %all-gather.6.cloned.1.call-update) | async-done | bytes 2097168 | tf_op jit(solution)/shard_map/all_gather | solution.py:140
  203.7 77.8 %all-gather.8.cloned.1.call-done = bf16[8192,128]{1,0:T(8,128)(2,1)} async-done(((bf16[256,128]{1,0:T(8,128)(2,1)}), bf16[8192,128]{1,0:T(8,128)(2,1)}) %all-gather.8.cloned.1.call-update) | async-done | bytes 2097168 | tf_op jit(solution)/shard_map/all_gather | solution.py:141
  281.5 15.4 %conditional.4 = (f32[1,8,64]{2,1,0:T(8,128)S(1)}, f32[1,8,64,128]{3,2,1,0:T(8,128)S(1)}) conditional(s32[]{:T(128)} %bitcast.73, () %tuple.48, (s32[8192]{0:T(1024)S(1)}, s32[256]{0:T(256)S(1)}, bf16[8192,1,128]{2,0,1:T(8,128)(2,1)}, bf16[256,1024]{1,0:T(8,128)(2,1)}, bf16[8192,1,128]{2,0,1:T(8,128)(2,1)}) %tuple.109), branch_computations={%region_6.7_spmd, %region_7.10_spmd} | conditional | flops 2202533376 | bytes 65450796 | solution.py:189
  281.5 0.3 broadcast_compare_fusion
  281.8 4.8 %fusion = (f32[8,64]{1,0:T(8,128)S(1)}, f32[8192,64,8]{0,1,2:T(8,128)S(1)}) fusion(pred[64,8192]{1,0:T(8,128)(4,1)S(1)} %broadcast_compare_fusion, bf16[8192,1,128]{2,0,1:T(8,128)(2,1)} %get-tuple-element.97, bf16[256,1024]{1,0:T(8,128)(2,1)} %get-tuple-element.98), kind=kOutput, calls=%fused_computation.4 | convolution fusion | flops 1086324224 | bytes 19531776 | tf_op jit(solution)/shard_map/cond/branch_1_fun/bgrd,kgd->grbk/dot_general | solution.py:164
  286.7 4.7 %fusion.10 = f32[1,8,64,128]{3,2,1,0:T(8,128)S(1)} fusion(bf16[8192,1,128]{2,0,1:T(8,128)(2,1)S(1)} %copy-done.2, f32[8192,64,8]{0,1,2:T(8,128)S(1)} %get-tuple-element.179, f32[8,64]{1,0:T(8,128)S(1)} %broadcast_maximum_fusion, pred[64,8192]{1,0:T(8,128)(4,1)S(1)} %broadcast_compare_fusion), kind=kOutput, calls=%fused_computation.13 | convolution fusion | flops 1094713344 | bytes 19662848 | tf_op jit(solution)/shard_map/cond/branch_1_fun/grbk,kgd->grbd/dot_general | solution.py:177
  291.4 5.5 %fusion.2 = f32[8,64]{1,0:T(8,128)S(1)} fusion(f32[8192,64,8]{0,1,2:T(8,128)S(1)} %get-tuple-element.179, f32[8,64]{1,0:T(8,128)S(1)} %broadcast_maximum_fusion, pred[64,8192]{1,0:T(8,128)(4,1)S(1)} %broadcast_compare_fusion), kind=kLoop, calls=%fused_computation.6 | loop fusion | flops 20971008 | bytes 17305600 | tf_op jit(solution)/shard_map/cond/branch_1_fun/reduce_sum | solution.py:176
  296.9 15.5 %conditional.5 = (f32[1,8,64]{2,1,0:T(8,128)S(1)}, f32[1,8,64,128]{3,2,1,0:T(8,128)S(1)}) conditional(s32[]{:T(128)} %bitcast.76, () %tuple.50, (s32[8192]{0:T(1024)S(1)}, s32[256]{0:T(256)S(1)}, bf16[8192,1,128]{2,0,1:T(8,128)(2,1)}, bf16[256,1024]{1,0:T(8,128)(2,1)}, bf16[8192,1,128]{2,0,1:T(8,128)(2,1)}) %tuple.110), branch_computations={%region_10.11_spmd, %region_11.14_spmd} | conditional | flops 2202533376 | bytes 65450796 | solution.py:189
  296.9 0.3 broadcast_compare_fusion.1
  297.3 4.9 %fusion.20 = (f32[8,64]{1,0:T(8,128)S(1)}, f32[8192,64,8]{0,1,2:T(8,128)S(1)}) fusion(pred[64,8192]{1,0:T(8,128)(4,1)S(1)} %broadcast_compare_fusion.1, bf16[8192,1,128]{2,0,1:T(8,128)(2,1)} %get-tuple-element.102, bf16[256,1024]{1,0:T(8,128)(2,1)} %get-tuple-element.103), kind=kOutput, calls=%fused_computation.24 | convolution fusion | flops 1086324224 | bytes 19531776 | tf_op jit(solution)/shard_map/cond/branch_1_fun/bgrd,kgd->grbk/dot_general | solution.py:164
  302.2 4.7 %fusion.30 = f32[1,8,64,128]{3,2,1,0:T(8,128)S(1)} fusion(bf16[8192,1,128]{2,0,1:T(8,128)(2,1)S(1)} %copy-done.3, f32[8192,64,8]{0,1,2:T(8,128)S(1)} %get-tuple-element.181, f32[8,64]{1,0:T(8,128)S(1)} %broadcast_maximum_fusion.1, pred[64,8192]{1,0:T(8,128)(4,1)S(1)} %broadcast_compare_fusion.1), kind=kOutput, calls=%fused_computation.33 | convolution fusion | flops 1094713344 | bytes 19662848 | tf_op jit(solution)/shard_map/cond/branch_1_fun/grbk,kgd->grbd/dot_general | solution.py:177
  306.9 5.5 %fusion.22 = f32[8,64]{1,0:T(8,128)S(1)} fusion(f32[8192,64,8]{0,1,2:T(8,128)S(1)} %get-tuple-element.181, f32[8,64]{1,0:T(8,128)S(1)} %broadcast_maximum_fusion.1, pred[64,8192]{1,0:T(8,128)(4,1)S(1)} %broadcast_compare_fusion.1), kind=kLoop, calls=%fused_computation.26 | loop fusion | flops 20971008 | bytes 17305600 | tf_op jit(solution)/shard_map/cond/branch_1_fun/reduce_sum | solution.py:176
  312.4 15.8 %conditional.6 = (f32[1,8,64]{2,1,0:T(8,128)S(1)}, f32[1,8,64,128]{3,2,1,0:T(8,128)S(1)}) conditional(s32[]{:T(128)} %bitcast.77, () %tuple.51, (s32[8192]{0:T(1024)S(1)}, s32[256]{0:T(256)S(1)}, bf16[8192,1,128]{2,0,1:T(8,128)(2,1)}, bf16[256,1024]{1,0:T(8,128)(2,1)}, bf16[8192,1,128]{2,0,1:T(8,128)(2,1)}) %tuple.111), branch_computations={%region_14.15_spmd, %region_15.18_spmd} | conditional | flops 2202533376 | bytes 65450796 | solution.py:189
  312.9 4.9 %fusion.40 = (f32[8,64]{1,0:T(8,128)S(1)}, f32[8192,64,8]{0,1,2:T(8,128)S(1)}) fusion(pred[64,8192]{1,0:T(8,128)(4,1)S(1)} %broadcast_compare_fusion.2, bf16[8192,1,128]{2,0,1:T(8,128)(2,1)} %get-tuple-element.107, bf16[256,1024]{1,0:T(8,128)(2,1)} %get-tuple-element.108), kind=kOutput, calls=%fused_computation.44 | convolution fusion | flops 1086324224 | bytes 19531776 | tf_op jit(solution)/shard_map/cond/branch_1_fun/bgrd,kgd->grbk/dot_general | solution.py:164
  317.8 4.8 %fusion.50 = f32[1,8,64,128]{3,2,1,0:T(8,128)S(1)} fusion(bf16[8192,1,128]{2,0,1:T(8,128)(2,1)S(1)} %copy-done.4, f32[8192,64,8]{0,1,2:T(8,128)S(1)} %get-tuple-element.183, f32[8,64]{1,0:T(8,128)S(1)} %broadcast_maximum_fusion.2, pred[64,8192]{1,0:T(8,128)(4,1)S(1)} %broadcast_compare_fusion.2), kind=kOutput, calls=%fused_computation.53 | convolution fusion | flops 1094713344 | bytes 19662848 | tf_op jit(solution)/shard_map/cond/branch_1_fun/grbk,kgd->grbd/dot_general | solution.py:177
  322.7 5.5 %fusion.42 = f32[8,64]{1,0:T(8,128)S(1)} fusion(f32[8192,64,8]{0,1,2:T(8,128)S(1)} %get-tuple-element.183, f32[8,64]{1,0:T(8,128)S(1)} %broadcast_maximum_fusion.2, pred[64,8192]{1,0:T(8,128)(4,1)S(1)} %broadcast_compare_fusion.2), kind=kLoop, calls=%fused_computation.46 | loop fusion | flops 20971008 | bytes 17305600 | tf_op jit(solution)/shard_map/cond/branch_1_fun/reduce_sum | solution.py:176
  328.1 15.5 %conditional.7 = (f32[1,8,64]{2,1,0:T(8,128)S(1)}, f32[1,8,64,128]{3,2,1,0:T(8,128)S(1)}) conditional(s32[]{:T(128)} %bitcast.78, () %tuple.52, (s32[8192]{0:T(1024)S(1)}, s32[256]{0:T(256)S(1)}, bf16[8192,1,128]{2,0,1:T(8,128)(2,1)}, bf16[256,1024]{1,0:T(8,128)(2,1)}, bf16[8192,1,128]{2,0,1:T(8,128)(2,1)}) %tuple.112), branch_computations={%region_18.19_spmd, %region_19.22_spmd} | conditional | flops 2202533376 | bytes 65450796 | solution.py:189
  328.2 0.3 broadcast_compare_fusion.3
  328.6 4.9 %fusion.60 = (f32[8,64]{1,0:T(8,128)S(1)}, f32[8192,64,8]{0,1,2:T(8,128)S(1)}) fusion(pred[64,8192]{1,0:T(8,128)(4,1)S(1)} %broadcast_compare_fusion.3, bf16[8192,1,128]{2,0,1:T(8,128)(2,1)} %get-tuple-element.112, bf16[256,1024]{1,0:T(8,128)(2,1)} %get-tuple-element.113), kind=kOutput, calls=%fused_computation.64 | convolution fusion | flops 1086324224 | bytes 19531776 | tf_op jit(solution)/shard_map/cond/branch_1_fun/bgrd,kgd->grbk/dot_general | solution.py:164
  333.5 4.7 %fusion.70 = f32[1,8,64,128]{3,2,1,0:T(8,128)S(1)} fusion(bf16[8192,1,128]{2,0,1:T(8,128)(2,1)S(1)} %copy-done.5, f32[8192,64,8]{0,1,2:T(8,128)S(1)} %get-tuple-element.185, f32[8,64]{1,0:T(8,128)S(1)} %broadcast_maximum_fusion.3, pred[64,8192]{1,0:T(8,128)(4,1)S(1)} %broadcast_compare_fusion.3), kind=kOutput, calls=%fused_computation.73 | convolution fusion | flops 1094713344 | bytes 19662848 | tf_op jit(solution)/shard_map/cond/branch_1_fun/grbk,kgd->grbd/dot_general | solution.py:177
  338.1 5.5 %fusion.62 = f32[8,64]{1,0:T(8,128)S(1)} fusion(f32[8192,64,8]{0,1,2:T(8,128)S(1)} %get-tuple-element.185, f32[8,64]{1,0:T(8,128)S(1)} %broadcast_maximum_fusion.3, pred[64,8192]{1,0:T(8,128)(4,1)S(1)} %broadcast_compare_fusion.3), kind=kLoop, calls=%fused_computation.66 | loop fusion | flops 20971008 | bytes 17305600 | tf_op jit(solution)/shard_map/cond/branch_1_fun/reduce_sum | solution.py:176
  343.7 0.4 fusion.102
  344.1 0.3 copy.89
  344.4 0.9 copy.124
  (55 shorter events, 2.0 us)
Async XLA Ops:
  7.2 118.8 %copy-start.1 = (f32[16]{0:T(128)S(1)}, f32[16]{0:T(128)}, u32[]{:S(2)}) copy-start(f32[16]{0:T(128)} %param.28) | copy-start | bytes 196
  7.2 119.8 %copy-start = (f32[1024]{0:T(1024)S(1)}, f32[1024]{0:T(1024)}, u32[]{:S(2)}) copy-start(f32[1024]{0:T(1024)} %param.31) | copy-start | bytes 12292
  7.2 118.7 %all-gather.10.cloned.1.call-start = ((), (), s32[]{:S(2)}) async-start(), calls=%async_computation.4 | async-start | bytes 8650752 | tf_op jit(solution)/shard_map/all_gather | solution.py:20
  8.2 16.1 %collective-permute-start = (bf16[3,1024]{0,1:T(8,128)(2,1)S(1)}, bf16[3,1024]{0,1:T(8,128)(2,1)S(1)}, u32[]{:S(2)}, u32[]{:S(2)}) collective-permute-start(bf16[3,1024]{0,1:T(8,128)(2,1)S(1)} %copy.76), channel_id=1, source_target_pairs={{0,8},{8,16},{16,24},{24,32},{32,40},{40,48},{48,56},{56,64},{64,7... | collective-permute-start | bytes 18440 | tf_op jit(solution)/shard_map/ppermute | solution.py:14
  12.7 10.1 %collective-permute-start.1 = (bf16[3,1,256]{2,0,1:T(4,128)(2,1)S(1)}, bf16[3,1,256]{2,0,1:T(4,128)(2,1)S(1)}, u32[]{:S(2)}, u32[]{:S(2)}) collective-permute-start(bf16[3,1,256]{2,0,1:T(4,128)(2,1)S(1)} %slice.125), channel_id=1, source_target_pairs={{0,8},{8,16},{16,24},{24,32},{32,40},{40,48},{48,56},{56,64},{64,7... | collective-permute-start | bytes 4616 | tf_op jit(solution)/shard_map/ppermute | solution.py:14
  26.8 176.9 %all-gather.6.cloned.1.call-start = ((), (), s32[]{:S(2)}) async-start(), calls=%async_computation.2 | async-start | bytes 2162688 | tf_op jit(solution)/shard_map/all_gather | solution.py:140
  27.5 254.0 %all-gather.8.cloned.1.call-start = ((), (), s32[]{:S(2)}) async-start(), calls=%async_computation.3 | async-start | bytes 2162688 | tf_op jit(solution)/shard_map/all_gather | solution.py:141
  28.3 317.1 %reduce-scatter.2.cloned.1.call-start = ((), (), s32[]{:S(2)}) async-start(), calls=%async_computation.1 | async-start | bytes 2359296 | tf_op jit(solution)/shard_map/reduce_scatter | solution.py:127
  281.5 5.2 %copy-start.2 = (bf16[8192,1,128]{2,0,1:T(8,128)(2,1)S(1)}, bf16[8192,1,128]{2,0,1:T(8,128)(2,1)}, u32[]{:S(2)}) copy-start(bf16[8192,1,128]{2,0,1:T(8,128)(2,1)} %get-tuple-element.99) | copy-start | bytes 6291460 | tf_op jit(solution)/shard_map/cond
  296.9 5.3 %copy-start.3 = (bf16[8192,1,128]{2,0,1:T(8,128)(2,1)S(1)}, bf16[8192,1,128]{2,0,1:T(8,128)(2,1)}, u32[]{:S(2)}) copy-start(bf16[8192,1,128]{2,0,1:T(8,128)(2,1)} %get-tuple-element.104) | copy-start | bytes 6291460 | tf_op jit(solution)/shard_map/cond
  312.6 5.3 %copy-start.4 = (bf16[8192,1,128]{2,0,1:T(8,128)(2,1)S(1)}, bf16[8192,1,128]{2,0,1:T(8,128)(2,1)}, u32[]{:S(2)}) copy-start(bf16[8192,1,128]{2,0,1:T(8,128)(2,1)} %get-tuple-element.109) | copy-start | bytes 6291460 | tf_op jit(solution)/shard_map/cond
  328.1 5.3 %copy-start.5 = (bf16[8192,1,128]{2,0,1:T(8,128)(2,1)S(1)}, bf16[8192,1,128]{2,0,1:T(8,128)(2,1)}, u32[]{:S(2)}) copy-start(bf16[8192,1,128]{2,0,1:T(8,128)(2,1)} %get-tuple-element.114) | copy-start | bytes 6291460 | tf_op jit(solution)/shard_map/cond
Sparse Core Ops, SparseCore 0:
  26.9 98.9 all-gather.9
  128.5 75.1 all-gather.5
  206.3 75.1 all-gather.7
  284.5 28.6 reduce-scatter.1
where the time goes:
time: 353 us; the launch traced here: 352 us
  waiting for transfers between devices  200 us (57%)
  matrix products  48.7 us (14%)
  blocking collectives  40.3 us (11%)
  other arithmetic  31.6 us (9%)
  between operations  16.4 us (5%)
  starting transfers between devices  7.79 us (2%)
  local copies, waits for them, and re-layouts  6.81 us (2%)
    all_gather x1, waiting for transfers between devices, per_device(): value_block = lax.all_gather(values, 'ctx', axis=0, tiled=True)  77.8 us
    all_gather x1, waiting for transfers between devices, per_device(): key_block = lax.all_gather(attention_keys, 'ctx', axis=0, tiled=True)  66.5 us
    all_gather x1, waiting for transfers between devices, prefix_2(): lax.all_gather(a.astype(kind), axis)  54.2 us
    all_gather x1, blocking collectives, prefix_2(): lax.all_gather(a.astype(kind), axis)  40.3 us
    reduce_sum x4, other arithmetic, update(): new_total = jnp.sum(weights, axis=3)  21.9 us
    dot_general x4, matrix products, update(): jnp.einsum('bgrd,kgd->grbk', query_tile_block, key_head_rows, preferred_e...  19.5 us
    dot_general x4, matrix products, update(): jnp.einsum('grbk,kgd->grbd', weights.astype(jnp.bfloat16), value_head_row...  18.8 us
    ppermute x2, starting transfers between devices, passed_along(): return lax.ppermute(shard, axis, pairs)  7.64 us
  transfers between devices with their start and end apart: 6, of which 3 were waited for; matrix products, arithmetic and copies ran while one was open for 24% of the time, Pallas kernels for 0%

commit v1 on v0

--- a/solution.py
+++ b/solution.py
@@ -137,7 +137,9 @@
     query_heads = queries.reshape(tok_rows, kv_heads, shared_heads, HEAD_SIZE)
     block_rows = tok_rows // 4
     first_key = jnp.int32(0)
-    key_block = lax.all_gather(attention_keys, "ctx", axis=0, tiled=True)
+    key_block = jnp.concatenate(
+        lax.all_to_all(jnp.stack([attention_keys] * lax.axis_size("ctx")), "ctx", 0, 0), axis=0
+    )
     value_block = lax.all_gather(values, "ctx", axis=0, tiled=True)
     key_count = key_block.shape[0]
     key_head_rows = key_block.reshape(key_count, kv_heads, HEAD_SIZE)

time: 353 us -> 291 us (0.82)
  waiting for transfers between devices: 200 us -> 75.4 us
  blocking collectives: 40.3 us -> 88.9 us
  starting transfers between devices: 7.79 us -> 17.6 us
    all_gather x1 -> x0, waiting for transfers between devices: 66.5 us -> none  [per_device(): key_block = lax.all_gather(attention_keys, 'ctx', axis=0, tiled=True)]
    all_gather x1, blocking collectives: 40.3 us -> 88.9 us  [prefix_2(): lax.all_gather(a.astype(kind), axis)]
    all_gather x1, waiting for transfers between devices: 54.2 us -> 8.53 us  [prefix_2(): lax.all_gather(a.astype(kind), axis)]
    all_gather x1, waiting for transfers between devices: 77.8 us -> 66.2 us  [per_device(): value_block = lax.all_gather(values, 'ctx', axis=0, tiled=True)]
    all_to_all x0 -> x1, starting transfers between devices: none -> 9.83 us  [per_device(): lax.all_to_all(jnp.stack([attention_keys] * lax.axis_size('ctx')), 'ctx',...]
  transfers between devices with their start and end apart: 6 -> 6, of which waited for: 3 -> 2; matrix products, arithmetic and copies ran while one was open for 24% -> 30% of each run, Pallas kernels for 0% -> 0%
where the time goes in v1:
time: 291 us; the launch traced here: 289 us
  blocking collectives  88.9 us (31%)
  waiting for transfers between devices  75.4 us (26%)
  matrix products  49.1 us (17%)
  other arithmetic  31.6 us (11%)
  starting transfers between devices  17.6 us (6%)
  between operations  16.4 us (6%)
  local copies, waits for them, and re-layouts  9.46 us (3%)
    all_gather x1, blocking collectives, prefix_2(): lax.all_gather(a.astype(kind), axis)  88.9 us
    all_gather x1, waiting for transfers between devices, per_device(): value_block = lax.all_gather(values, 'ctx', axis=0, tiled=True)  66.2 us
    reduce_sum x4, other arithmetic, update(): new_total = jnp.sum(weights, axis=3)  21.9 us
    dot_general x4, matrix products, update(): jnp.einsum('grbk,kgd->grbd', weights.astype(jnp.bfloat16), value_head_row...  18.9 us
    dot_general x4, matrix products, update(): jnp.einsum('bgrd,kgd->grbk', query_tile_block, key_head_rows, preferred_e...  17.2 us
    all_to_all x1, starting transfers between devices, per_device(): lax.all_to_all(jnp.stack([attention_keys] * lax.axis_size('ctx')), 'ctx',...  9.83 us
    all_gather x1, waiting for transfers between devices, prefix_2(): lax.all_gather(a.astype(kind), axis)  8.53 us
    ppermute x2, starting transfers between devices, passed_along(): return lax.ppermute(shard, axis, pairs)  7.65 us
  transfers between devices with their start and end apart: 6, of which 2 were waited for; matrix products, arithmetic and copies ran while one was open for 30% of the time, Pallas kernels for 0%

profile of v1, /device:TPU:4, one launch (start us, length us, event | category | flops | bytes accessed | tf_op | source)
XLA Modules:
  0.0 288.9 jit_solution(8687275468281543021)
XLA Ops:
  7.2 0.7 slice.125
  7.9 3.8 %collective-permute-start.1 = (bf16[3,1,256]{2,0,1:T(4,128)(2,1)S(1)}, bf16[3,1,256]{2,0,1:T(4,128)(2,1)S(1)}, u32[]{:S(2)}, u32[]{:S(2)}) collective-permute-start(bf16[3,1,256]{2,0,1:T(4,128)(2,1)S(1)} %slice.125), channel_id=1, source_target_pairs={{0,8},{8,16},{16,24},{24,32},{32,40},{40,48},{48,56},{56,64},{64,7... | collective-permute-start | bytes 4616 | tf_op jit(solution)/shard_map/ppermute | solution.py:14
  11.7 0.7 slice.117
  12.7 3.8 %collective-permute-start = (bf16[3,1024]{0,1:T(8,128)(2,1)S(1)}, bf16[3,1024]{0,1:T(8,128)(2,1)S(1)}, u32[]{:S(2)}, u32[]{:S(2)}) collective-permute-start(bf16[3,1024]{0,1:T(8,128)(2,1)S(1)} %copy.76), channel_id=1, source_target_pairs={{0,8},{8,16},{16,24},{24,32},{32,40},{40,48},{48,56},{56,64},{64,7... | collective-permute-start | bytes 18440 | tf_op jit(solution)/shard_map/ppermute | solution.py:14
  16.5 0.7 exponential_negate_fusion
  17.2 0.8 compare_select_fusion
  18.0 0.6 reduce-window.6
  18.8 0.9 slice_convert_fusion.3
  19.9 0.8 multiply_bitcast_fusion
  20.7 0.8 slice_convert_fusion.7
  21.6 1.3 copy.77
  22.8 1.4 multiply_convert_fusion.7
  24.3 1.5 fusion.96
  25.8 1.0 convolution_convert_fusion.1
  26.8 0.7 all-gather.5.cloned.1.call-update
  27.5 2.6 stack.2
  30.2 9.8 %all-to-all-start = ((bf16[32,256,128]{2,1,0:T(8,128)(2,1)}), bf16[32,256,128]{2,1,0:T(8,128)(2,1)S(1)}, u32[]{:S(2)}, u32[]{:S(2)}) async-start(bf16[32,256,128]{2,1,0:T(8,128)(2,1)} %stack.2), calls=%async_computation.1 | async-start | bytes 4194304 | tf_op jit(solution)/shard_map/all_to_all | solution.py:141
  40.1 88.9 %all-gather = bf16[32,16,1]{1,2,0:T(2,128)(2,1)S(1)} all-gather(bf16[1,16,1]{1,2,0:T(2,128)(2,1)S(1)} %slice.213), channel_id=2, replica_groups=mesh['ctx'=32,'tp'=8] {'ctx'}, dimensions={0}, use_global_device_ids=true | all-gather | bytes 1056 | tf_op jit(solution)/shard_map/all_gather | solution.py:20
  129.3 1.2 copy.88
  130.7 2.6 fusion.87
  133.3 8.5 %all-gather.7.cloned.1.call-done = bf16[512,64,128]{2,1,0:T(8,128)(2,1)} async-done(((bf16[16,64,128]{2,1,0:T(8,128)(2,1)}), bf16[512,64,128]{2,1,0:T(8,128)(2,1)}) %all-gather.7.cloned.1.call-update) | async-done | bytes 8388624 | tf_op jit(solution)/shard_map/all_gather | solution.py:20
  141.9 2.0 fusion.90
  143.9 0.4 multiply_reduce_fusion
  144.3 7.2 %convolution_convert_fusion = bf16[256,4096]{1,0:T(8,128)(2,1)} fusion(bf16[1024,4096]{1,0:T(8,128)(2,1)} %param.32, f32[256,1024]{0,1:T(8,128)S(1)} %get-tuple-element.171, f32[1024]{0:T(1024)S(1)} %copy-done.1, f32[256]{0:T(256)S(1)} %add_rsqrt_fusion), kind=kOutput, calls=%fused_computation.82 | convolution fusion | flops 2149318656 | bytes 11539456 | tf_op jit(solution)/shard_map/dot_general | solution.py:128
  151.5 0.6 fusion.116
  154.6 66.2 %all-gather.5.cloned.1.call-done = bf16[8192,128]{1,0:T(8,128)(2,1)} async-done(((bf16[256,128]{1,0:T(8,128)(2,1)}), bf16[8192,128]{1,0:T(8,128)(2,1)}) %all-gather.5.cloned.1.call-update) | async-done | bytes 2097168 | tf_op jit(solution)/shard_map/all_gather | solution.py:143
  220.8 14.9 %conditional.7 = (f32[1,8,64]{2,1,0:T(8,128)S(1)}, f32[1,8,64,128]{3,2,1,0:T(8,128)S(1)}) conditional(s32[]{:T(128)} %bitcast.78, () %tuple.52, (s32[8192]{0:T(1024)S(1)}, s32[256]{0:T(256)S(1)}, bf16[8192,1,128]{2,0,1:T(8,128)(2,1)S(1)}, bf16[256,1024]{1,0:T(8,128)(2,1)}, bf16[8192,1,128]{2,0,1:T(8,128)(2,1)}) %tuple.107), branch_computations={%region_18.19_spmd, %region_19.22_spmd} | conditional | flops 2202533376 | bytes 65450796 | solution.py:191
  220.9 0.3 broadcast_compare_fusion.3
  221.2 4.3 %fusion.60 = (f32[8,64]{1,0:T(8,128)S(1)}, f32[8192,64,8]{0,1,2:T(8,128)S(1)}) fusion(pred[64,8192]{1,0:T(8,128)(4,1)S(1)} %broadcast_compare_fusion.3, bf16[8192,1,128]{2,0,1:T(8,128)(2,1)S(1)} %get-tuple-element.112, bf16[256,1024]{1,0:T(8,128)(2,1)} %get-tuple-element.113), kind=kOutput, calls=%fused_computation.64 | convolution fusion | flops 1086324224 | bytes 19531776 | tf_op jit(solution)/shard_map/cond/branch_1_fun/bgrd,kgd->grbk/dot_general | solution.py:166
  225.5 4.7 %fusion.70 = f32[1,8,64,128]{3,2,1,0:T(8,128)S(1)} fusion(bf16[8192,1,128]{2,0,1:T(8,128)(2,1)S(1)} %copy-done.3, f32[8192,64,8]{0,1,2:T(8,128)S(1)} %get-tuple-element.185, f32[8,64]{1,0:T(8,128)S(1)} %broadcast_maximum_fusion.3, pred[64,8192]{1,0:T(8,128)(4,1)S(1)} %broadcast_compare_fusion.3), kind=kOutput, calls=%fused_computation.73 | convolution fusion | flops 1094713344 | bytes 19662848 | tf_op jit(solution)/shard_map/cond/branch_1_fun/grbk,kgd->grbd/dot_general | solution.py:179
  230.2 5.5 %fusion.62 = f32[8,64]{1,0:T(8,128)S(1)} fusion(f32[8192,64,8]{0,1,2:T(8,128)S(1)} %get-tuple-element.185, f32[8,64]{1,0:T(8,128)S(1)} %broadcast_maximum_fusion.3, pred[64,8192]{1,0:T(8,128)(4,1)S(1)} %broadcast_compare_fusion.3), kind=kLoop, calls=%fused_computation.66 | loop fusion | flops 20971008 | bytes 17305600 | tf_op jit(solution)/shard_map/cond/branch_1_fun/reduce_sum | solution.py:178
  235.7 14.8 %conditional.6 = (f32[1,8,64]{2,1,0:T(8,128)S(1)}, f32[1,8,64,128]{3,2,1,0:T(8,128)S(1)}) conditional(s32[]{:T(128)} %bitcast.77, () %tuple.51, (s32[8192]{0:T(1024)S(1)}, s32[256]{0:T(256)S(1)}, bf16[8192,1,128]{2,0,1:T(8,128)(2,1)S(1)}, bf16[256,1024]{1,0:T(8,128)(2,1)}, bf16[8192,1,128]{2,0,1:T(8,128)(2,1)}) %tuple.108), branch_computations={%region_14.15_spmd, %region_15.18_spmd} | conditional | flops 2202533376 | bytes 65450796 | solution.py:191
  235.7 0.3 broadcast_compare_fusion.2
  236.1 4.3 %fusion.40 = (f32[8,64]{1,0:T(8,128)S(1)}, f32[8192,64,8]{0,1,2:T(8,128)S(1)}) fusion(pred[64,8192]{1,0:T(8,128)(4,1)S(1)} %broadcast_compare_fusion.2, bf16[8192,1,128]{2,0,1:T(8,128)(2,1)S(1)} %get-tuple-element.107, bf16[256,1024]{1,0:T(8,128)(2,1)} %get-tuple-element.108), kind=kOutput, calls=%fused_computation.44 | convolution fusion | flops 1086324224 | bytes 19531776 | tf_op jit(solution)/shard_map/cond/branch_1_fun/bgrd,kgd->grbk/dot_general | solution.py:166
  240.4 4.7 %fusion.50 = f32[1,8,64,128]{3,2,1,0:T(8,128)S(1)} fusion(bf16[8192,1,128]{2,0,1:T(8,128)(2,1)S(1)} %copy-done.4, f32[8192,64,8]{0,1,2:T(8,128)S(1)} %get-tuple-element.183, f32[8,64]{1,0:T(8,128)S(1)} %broadcast_maximum_fusion.2, pred[64,8192]{1,0:T(8,128)(4,1)S(1)} %broadcast_compare_fusion.2), kind=kOutput, calls=%fused_computation.53 | convolution fusion | flops 1094713344 | bytes 19662848 | tf_op jit(solution)/shard_map/cond/branch_1_fun/grbk,kgd->grbd/dot_general | solution.py:179
  245.1 5.5 %fusion.42 = f32[8,64]{1,0:T(8,128)S(1)} fusion(f32[8192,64,8]{0,1,2:T(8,128)S(1)} %get-tuple-element.183, f32[8,64]{1,0:T(8,128)S(1)} %broadcast_maximum_fusion.2, pred[64,8192]{1,0:T(8,128)(4,1)S(1)} %broadcast_compare_fusion.2), kind=kLoop, calls=%fused_computation.46 | loop fusion | flops 20971008 | bytes 17305600 | tf_op jit(solution)/shard_map/cond/branch_1_fun/reduce_sum | solution.py:178
  250.5 15.4 %conditional.5 = (f32[1,8,64]{2,1,0:T(8,128)S(1)}, f32[1,8,64,128]{3,2,1,0:T(8,128)S(1)}) conditional(s32[]{:T(128)} %bitcast.76, () %tuple.50, (s32[8192]{0:T(1024)S(1)}, s32[256]{0:T(256)S(1)}, bf16[8192,1,128]{2,0,1:T(8,128)(2,1)S(1)}, bf16[256,1024]{1,0:T(8,128)(2,1)}, bf16[8192,1,128]{2,0,1:T(8,128)(2,1)}) %tuple.109), branch_computations={%region_10.11_spmd, %region_11.14_spmd} | conditional | flops 2202533376 | bytes 65450796 | solution.py:191
  251.1 4.3 %fusion.20 = (f32[8,64]{1,0:T(8,128)S(1)}, f32[8192,64,8]{0,1,2:T(8,128)S(1)}) fusion(pred[64,8192]{1,0:T(8,128)(4,1)S(1)} %broadcast_compare_fusion.1, bf16[8192,1,128]{2,0,1:T(8,128)(2,1)S(1)} %get-tuple-element.102, bf16[256,1024]{1,0:T(8,128)(2,1)} %get-tuple-element.103), kind=kOutput, calls=%fused_computation.24 | convolution fusion | flops 1086324224 | bytes 19531776 | tf_op jit(solution)/shard_map/cond/branch_1_fun/bgrd,kgd->grbk/dot_general | solution.py:166
  255.5 4.9 %fusion.30 = f32[1,8,64,128]{3,2,1,0:T(8,128)S(1)} fusion(bf16[8192,1,128]{2,0,1:T(8,128)(2,1)S(1)} %copy-done.5, f32[8192,64,8]{0,1,2:T(8,128)S(1)} %get-tuple-element.181, f32[8,64]{1,0:T(8,128)S(1)} %broadcast_maximum_fusion.1, pred[64,8192]{1,0:T(8,128)(4,1)S(1)} %broadcast_compare_fusion.1), kind=kOutput, calls=%fused_computation.33 | convolution fusion | flops 1094713344 | bytes 19662848 | tf_op jit(solution)/shard_map/cond/branch_1_fun/grbk,kgd->grbd/dot_general | solution.py:179
  260.4 5.5 %fusion.22 = f32[8,64]{1,0:T(8,128)S(1)} fusion(f32[8192,64,8]{0,1,2:T(8,128)S(1)} %get-tuple-element.181, f32[8,64]{1,0:T(8,128)S(1)} %broadcast_maximum_fusion.1, pred[64,8192]{1,0:T(8,128)(4,1)S(1)} %broadcast_compare_fusion.1), kind=kLoop, calls=%fused_computation.26 | loop fusion | flops 20971008 | bytes 17305600 | tf_op jit(solution)/shard_map/cond/branch_1_fun/reduce_sum | solution.py:178
  265.9 14.8 %conditional.4 = (f32[1,8,64]{2,1,0:T(8,128)S(1)}, f32[1,8,64,128]{3,2,1,0:T(8,128)S(1)}) conditional(s32[]{:T(128)} %bitcast.73, () %tuple.48, (s32[8192]{0:T(1024)S(1)}, s32[256]{0:T(256)S(1)}, bf16[8192,1,128]{2,0,1:T(8,128)(2,1)S(1)}, bf16[256,1024]{1,0:T(8,128)(2,1)}, bf16[8192,1,128]{2,0,1:T(8,128)(2,1)}) %tuple.110), branch_computations={%region_6.7_spmd, %region_7.10_spmd} | conditional | flops 2202533376 | bytes 65450796 | solution.py:191
  265.9 0.3 broadcast_compare_fusion
  266.3 4.3 %fusion = (f32[8,64]{1,0:T(8,128)S(1)}, f32[8192,64,8]{0,1,2:T(8,128)S(1)}) fusion(pred[64,8192]{1,0:T(8,128)(4,1)S(1)} %broadcast_compare_fusion, bf16[8192,1,128]{2,0,1:T(8,128)(2,1)S(1)} %get-tuple-element.97, bf16[256,1024]{1,0:T(8,128)(2,1)} %get-tuple-element.98), kind=kOutput, calls=%fused_computation.4 | convolution fusion | flops 1086324224 | bytes 19531776 | tf_op jit(solution)/shard_map/cond/branch_1_fun/bgrd,kgd->grbk/dot_general | solution.py:166
  270.6 4.7 %fusion.10 = f32[1,8,64,128]{3,2,1,0:T(8,128)S(1)} fusion(bf16[8192,1,128]{2,0,1:T(8,128)(2,1)S(1)} %copy-done.6, f32[8192,64,8]{0,1,2:T(8,128)S(1)} %get-tuple-element.179, f32[8,64]{1,0:T(8,128)S(1)} %broadcast_maximum_fusion, pred[64,8192]{1,0:T(8,128)(4,1)S(1)} %broadcast_compare_fusion), kind=kOutput, calls=%fused_computation.13 | convolution fusion | flops 1094713344 | bytes 19662848 | tf_op jit(solution)/shard_map/cond/branch_1_fun/grbk,kgd->grbd/dot_general | solution.py:179
  275.2 5.5 %fusion.2 = f32[8,64]{1,0:T(8,128)S(1)} fusion(f32[8192,64,8]{0,1,2:T(8,128)S(1)} %get-tuple-element.179, f32[8,64]{1,0:T(8,128)S(1)} %broadcast_maximum_fusion, pred[64,8192]{1,0:T(8,128)(4,1)S(1)} %broadcast_compare_fusion), kind=kLoop, calls=%fused_computation.6 | loop fusion | flops 20971008 | bytes 17305600 | tf_op jit(solution)/shard_map/cond/branch_1_fun/reduce_sum | solution.py:178
  280.8 0.4 fusion.102
  281.2 0.3 copy.89
  281.5 0.9 copy.124
  (57 shorter events, 2.0 us)
Async XLA Ops:
  7.2 134.8 %copy-start.2 = (f32[16]{0:T(128)S(1)}, f32[16]{0:T(128)}, u32[]{:S(2)}) copy-start(f32[16]{0:T(128)} %param.28) | copy-start | bytes 196
  7.2 134.7 %all-gather.7.cloned.1.call-start = ((), (), s32[]{:S(2)}) async-start(), calls=%async_computation.4 | async-start | bytes 8650752 | tf_op jit(solution)/shard_map/all_gather | solution.py:20
  7.9 14.9 %collective-permute-start.1 = (bf16[3,1,256]{2,0,1:T(4,128)(2,1)S(1)}, bf16[3,1,256]{2,0,1:T(4,128)(2,1)S(1)}, u32[]{:S(2)}, u32[]{:S(2)}) collective-permute-start(bf16[3,1,256]{2,0,1:T(4,128)(2,1)S(1)} %slice.125), channel_id=1, source_target_pairs={{0,8},{8,16},{16,24},{24,32},{32,40},{40,48},{48,56},{56,64},{64,7... | collective-permute-start | bytes 4616 | tf_op jit(solution)/shard_map/ppermute | solution.py:14
  12.7 11.6 %collective-permute-start = (bf16[3,1024]{0,1:T(8,128)(2,1)S(1)}, bf16[3,1024]{0,1:T(8,128)(2,1)S(1)}, u32[]{:S(2)}, u32[]{:S(2)}) collective-permute-start(bf16[3,1024]{0,1:T(8,128)(2,1)S(1)} %copy.76), channel_id=1, source_target_pairs={{0,8},{8,16},{16,24},{24,32},{32,40},{40,48},{48,56},{56,64},{64,7... | collective-permute-start | bytes 18440 | tf_op jit(solution)/shard_map/ppermute | solution.py:14
  21.6 122.7 %copy-start.1 = (f32[1024]{0:T(1024)S(1)}, f32[1024]{0:T(1024)}, u32[]{:S(2)}) copy-start(f32[1024]{0:T(1024)} %param.31) | copy-start | bytes 12292
  25.8 116.1 %copy-start = (bf16[256,1024]{0,1:T(8,128)(2,1)}, bf16[256,1024]{0,1:T(8,128)(2,1)S(1)}, u32[]{:S(2)}) copy-start(bf16[256,1024]{0,1:T(8,128)(2,1)S(1)} %get-tuple-element.175) | copy-start | bytes 1572868
  26.8 194.0 %all-gather.5.cloned.1.call-start = ((), (), s32[]{:S(2)}) async-start(), calls=%async_computation.3 | async-start | bytes 2162688 | tf_op jit(solution)/shard_map/all_gather | solution.py:143
  30.2 190.6 %all-to-all-start = ((bf16[32,256,128]{2,1,0:T(8,128)(2,1)}), bf16[32,256,128]{2,1,0:T(8,128)(2,1)S(1)}, u32[]{:S(2)}, u32[]{:S(2)}) async-start(bf16[32,256,128]{2,1,0:T(8,128)(2,1)} %stack.2), calls=%async_computation.1 | async-start | bytes 4194304 | tf_op jit(solution)/shard_map/all_to_all | solution.py:141
  40.0 242.4 %reduce-scatter.2.cloned.1.call-start = ((), (), s32[]{:S(2)}) async-start(), calls=%async_computation.2 | async-start | bytes 2359296 | tf_op jit(solution)/shard_map/reduce_scatter | solution.py:127
  220.8 4.7 %copy-start.3 = (bf16[8192,1,128]{2,0,1:T(8,128)(2,1)S(1)}, bf16[8192,1,128]{2,0,1:T(8,128)(2,1)}, u32[]{:S(2)}) copy-start(bf16[8192,1,128]{2,0,1:T(8,128)(2,1)} %get-tuple-element.114) | copy-start | bytes 6291460 | tf_op jit(solution)/shard_map/cond
  235.7 4.7 %copy-start.4 = (bf16[8192,1,128]{2,0,1:T(8,128)(2,1)S(1)}, bf16[8192,1,128]{2,0,1:T(8,128)(2,1)}, u32[]{:S(2)}) copy-start(bf16[8192,1,128]{2,0,1:T(8,128)(2,1)} %get-tuple-element.109) | copy-start | bytes 6291460 | tf_op jit(solution)/shard_map/cond
  250.7 4.8 %copy-start.5 = (bf16[8192,1,128]{2,0,1:T(8,128)(2,1)S(1)}, bf16[8192,1,128]{2,0,1:T(8,128)(2,1)}, u32[]{:S(2)}) copy-start(bf16[8192,1,128]{2,0,1:T(8,128)(2,1)} %get-tuple-element.104) | copy-start | bytes 6291460 | tf_op jit(solution)/shard_map/cond
  265.9 4.7 %copy-start.6 = (bf16[8192,1,128]{2,0,1:T(8,128)(2,1)S(1)}, bf16[8192,1,128]{2,0,1:T(8,128)(2,1)}, u32[]{:S(2)}) copy-start(bf16[8192,1,128]{2,0,1:T(8,128)(2,1)} %get-tuple-element.99) | copy-start | bytes 6291460 | tf_op jit(solution)/shard_map/cond
Sparse Core Ops, SparseCore 0:
  26.9 114.8 all-gather.6
  144.4 76.2 all-gather.4
  223.9 28.5 reduce-scatter.1
